TPU v7x, 256 devices: a whole 4x4x8 slice. The times are simulated.
256 devices in a mesh: gx: 4 (over y), yz: 64 (over z, x, core).
Axes of the slice: x: 4, y: 4, z: 8, core: 2. Of those that a mesh axis runs over, the one named last changes fastest.
Arguments:
- spin_vectors: float32 [3, 2, 16, 128, 128], P(None, None, 'gx', 'yz'), may hold values from -1 to 1, as said below
- pair_weight: float32 [112, 128], replicated, may hold values from -0.5 to 0.5
- mix_weight: float32 [128, 128], replicated, may hold values from -0.5 to 0.5
- mix_bias: float32 [128], replicated, may hold values from -3 to 3
- out_weight: float32 [128], replicated, may hold values from -0.5 to 0.5
Outputs:
- spins_next: float32 [3, 2, 16, 128, 128], P(None, None, 'gx', 'yz')
- field_next: float32 [3, 2, 16, 128, 128], P(None, None, 'gx', 'yz')
Inputs may be any that keep to these rules, and one draw needn't show every extreme that they name: `spin_vectors`: every atom's spin has unit length.
All inputs are finite; a program needn't handle non-finite values.
Results may differ from a plain program's by a relative error of at most 0.0003.
Values sent between devices are 32-bit elements; how exact they have to be, the bound alone decides.
A program may use at most 128 MiB of HBM per device.

v0:
```python
import functools

import jax
import jax.numpy as jnp
from jax import lax
from jax.experimental import pallas as pl
from jax.experimental.pallas import tpu as pltpu
from jax.sharding import PartitionSpec as P

MESH = pl.DeviceIdType.MESH
NB = 8
NXI = 6
NT = 2 * NXI * 8
TIME_STEP = 0.1
CHUNK = 4
F32 = jnp.float32
BF16 = jnp.bfloat16

FIRST = [(i, j, k) for i in (-1, 0) for j in (-1, 0) for k in (-1, 0)]
SECOND = [(1, 0, 0), (-1, 0, 0), (0, 1, 0), (0, -1, 0), (0, 0, 1), (0, 0, -1)]
DELTAS = (1, -1, 2, -2)
GX_DELTAS = (0, 1, -1, 2, -2)


def bond_list(sub):
    sign = 1 - 2 * sub
    result = [(1 - sub, sign * i, sign * j, sign * k) for i, j, k in FIRST]
    return result + [(sub, i, j, k) for i, j, k in SECOND]


BONDS = (bond_list(0), bond_list(1))


def partner(o):
    return o if o < 8 else 8 + ((o - 8) ^ 1)


def row_shift(sub, target, dy):
    return dy + target - sub


def with_neighbours(atoms):
    result = set(atoms)
    for sub, x, y, z in atoms:
        for target, dx, dy, dz in BONDS[sub]:
            result.add((target, x + dx, y + dy, z + dz))
    return result


def columns_of(atoms):
    return sorted({atom[:3] for atom in atoms})


MAIN = columns_of(with_neighbours([(s, x, 0, 0) for s in (0, 1) for x in (0, 1)]))
LOW_SIDE = columns_of(with_neighbours([(1, x, -2, 63) for x in (0, 1)]))
HIGH_SIDE = columns_of(with_neighbours([(0, x, 2, 0) for x in (0, 1)]))
LOW_SIDE = [c for c in LOW_SIDE if c not in MAIN]
HIGH_SIDE = [c for c in HIGH_SIDE if c not in MAIN]
FINAL = columns_of(
    with_neighbours([(s, x, y, 0) for s in (0, 1) for x in range(4) for y in (0, 1)])
)


def tile(sub, xi, slot, half):
    return half * NT + (sub * NXI + xi) * 8 + slot


def column_tile(column, half):
    sub, x, y = column
    return tile(sub, x + 1, y + 3 + sub, half)


def rolled(value, dz):
    return value if dz == 0 else pltpu.roll(value, (-dz) % 128, value.ndim - 1)


def kernel(
    n_gx,
    n_yz,
    spin_ref,
    pair_ref,
    mix_ref,
    bias_ref,
    out_w_ref,
    spin_out,
    field_out,
    state,
    cosine,
    slope,
    first_w,
    second_w,
    scratch_w,
    start_yz,
    start_gx,
    send_buf,
    got_yz,
    got_gx,
    start_send,
    start_recv,
    send_sem,
    recv_yz,
    recv_gx,
):
    gx = lax.axis_index("gx")
    yz = lax.axis_index("yz")

    def device(dgx, dyz):
        return (lax.rem(gx + dgx + n_gx, n_gx), lax.rem(yz + dyz + n_yz, n_yz))

    barrier = pltpu.get_barrier_semaphore()
    partners = [(0, d) for d in DELTAS] + [(s, d) for s in (1, -1) for d in GX_DELTAS]
    for dgx, dyz in partners:
        pl.semaphore_signal(barrier, inc=1, device_id=device(dgx, dyz), device_id_type=MESH)

    scratch_w[...] = jnp.zeros((128, 128), F32)
    for k in range(NB):
        scratch_w[16 * k : 16 * k + 8, :] = pair_ref[pl.ds(k, 8, stride=8), :]
        scratch_w[16 * k + 8 : 16 * k + 14, :] = pair_ref[pl.ds(64 + k, 6, stride=8), :]
    merged = jnp.dot(
        scratch_w[...],
        mix_ref[...],
        precision=lax.Precision.HIGHEST,
        preferred_element_type=F32,
    )
    row = lax.broadcasted_iota(jnp.int32, (128, 128), 0)
    with_bias = jnp.where(row == 14, jnp.broadcast_to(bias_ref[...], (128, 128)), merged)
    degree = (row // 16 + 1).astype(F32)
    scaled = -merged * degree * jnp.broadcast_to(out_w_ref[...], (128, 128))

    def stacked(matrix):
        high = matrix.astype(BF16)
        low = (matrix - high.astype(F32)).astype(BF16)
        return jnp.concatenate(
            [jnp.concatenate([high, high], 1), jnp.concatenate([low, low], 1)], 0
        )

    first_w[...] = stacked(with_bias.T)
    second_w[...] = stacked(scaled)
    cosine[...] = jnp.ones(cosine.shape, F32)
    slope[...] = jnp.zeros(slope.shape, F32)
    state[...] = jnp.zeros(state.shape, F32)

    pl.semaphore_wait(barrier, len(partners))

    starts = []
    for j, d in enumerate(DELTAS):
        starts.append(
            pltpu.make_async_remote_copy(
                src_ref=spin_ref,
                dst_ref=start_yz.at[j],
                send_sem=start_send.at[j],
                recv_sem=start_recv.at[j],
                device_id=device(0, d),
                device_id_type=MESH,
            )
        )
    for j, d in enumerate(GX_DELTAS):
        starts.append(
            pltpu.make_async_remote_copy(
                src_ref=spin_ref.at[:, :, 2:4],
                dst_ref=start_gx.at[j],
                send_sem=start_send.at[4 + j],
                recv_sem=start_recv.at[4 + j],
                device_id=device(1, d),
                device_id_type=MESH,
            )
        )
    for copy in starts:
        copy.start()

    def put(value_of_sub, first_x, count, y, rows):
        for sub in (0, 1):
            r = y + 4 + sub
            state[1, :, sub, pl.ds(first_x, count), r : r + rows, :] = value_of_sub(sub)

    def roll_all(first_x, count):
        for sub in (0, 1):
            value = state[1, :, sub, pl.ds(first_x, count), :, :]
            state[0, :, sub, pl.ds(first_x, count), :, :] = rolled(value, -1)
            state[2, :, sub, pl.ds(first_x, count), :, :] = rolled(value, 1)

    put(lambda sub: spin_ref[:, sub], 2, 4, 0, 2)
    for copy in starts:
        copy.wait()
    for j, d in enumerate(DELTAS):
        put(lambda sub: start_yz[j, :, sub], 2, 4, -2 * d, 2)
    for j, d in enumerate(GX_DELTAS):
        put(lambda sub: start_gx[j, :, sub], 0, 2, -2 * d, 2)
    roll_all(0, 6)

    def cosines(first_x, count, y0):
        r0 = 1 + y0
        for sub in (0, 1):
            centre = state[1, :, sub, pl.ds(first_x, count), r0 : r0 + 8, :]
            for o, (target, dx, dy, dz) in enumerate(BONDS[sub]):
                r = r0 + row_shift(sub, target, dy)
                other = state[1 + dz, :, target, pl.ds(first_x + dx, count), r : r + 8, :]
                product = centre * other
                value = product[0] + product[1] + product[2]
                for xi in range(count):
                    at = tile(sub, xi, 0, o // 8) * 8 + o % 8
                    cosine[pl.ds(at, 8, stride=8), :] = value[xi]

    def load_cosine(column):
        halves = []
        for half in (0, 1):
            at = column_tile(column, half) * 8
            halves.append(cosine[at : at + 8, :])
        return jnp.concatenate(halves, 0)

    def store_slope(column, value):
        for half in (0, 1):
            at = column_tile(column, half) * 8 + 8
            slope[at : at + 8, :] = value[8 * half : 8 * half + 8, :]

    def product(weight, value):
        high = value.astype(BF16)
        low = (value - high.astype(F32)).astype(BF16)
        wide = jnp.dot(
            weight[...], jnp.concatenate([high, low], 0), preferred_element_type=F32
        )
        return wide[:128] + wide[128:]

    def network(values):
        results = []
        for begin in range(0, len(values), CHUNK):
            part = values[begin : begin + CHUNK]
            c = jnp.concatenate(part, 1)
            twice = c + c
            firsts = [jnp.ones_like(c), c]
            seconds = [jnp.ones_like(c), twice]
            for _ in range(2, NB + 1):
                firsts.append(twice * firsts[-1] - firsts[-2])
                seconds.append(twice * seconds[-1] - seconds[-2])
            u = jnp.tanh(product(first_w, jnp.concatenate(firsts[1:], 0)))
            d = product(second_w, 1.0 - u * u)
            g = d[0:16]
            for k in range(1, NB):
                g = g + d[16 * k : 16 * k + 16] * seconds[k]
            results += [g[:, 128 * j : 128 * j + 128] for j in range(len(part))]
        return results

    lane = lax.broadcasted_iota(jnp.int32, (16, 128), 1)

    def packed(groups):
        result = None
        for first, columns in groups:
            order = lax.rem(lane + (256 - first), 128)
            for m, column in enumerate(columns):
                value = load_cosine(column)
                if m:
                    value = pltpu.roll(value, 4 * m, 1)
                if result is None:
                    result = value
                else:
                    inside = (order >= 4 * m) & (order < 4 * m + 4)
                    result = jnp.where(inside, value, result)
        return result

    def packed_pair(columns):
        result = None
        low = lax.rem(lane + (256 - 63), 128)
        high = lax.rem(lane + (256 - 125), 128)
        for m, column in enumerate(columns):
            value = load_cosine(column)
            if m:
                value = pltpu.roll(value, 4 * m, 1)
                inside = ((low >= 4 * m) & (low < 4 * m + 4)) | (
                    (high >= 4 * m) & (high < 4 * m + 4)
                )
                value = jnp.where(inside, value, result)
            result = value
        return result

    def spread(value, columns):
        for m, column in enumerate(columns):
            store_slope(column, pltpu.roll(value, 128 - 4 * m, 1) if m else value)

    def fields(sub, xi0, count, first_x, y0):
        r0 = 1 + y0
        total = None
        for o, (target, dx, dy, dz) in enumerate(BONDS[sub]):
            mate = partner(o)
            shift = row_shift(sub, target, dy)
            coefficients = []
            for xi in range(xi0, xi0 + count):
                at = (tile(sub, xi, 0, o // 8) + 1) * 8 + o % 8
                own = slope[pl.ds(at, 8, stride=8), :]
                at = (tile(target, xi + dx, shift, mate // 8) + 1) * 8 + mate % 8
                theirs = slope[pl.ds(at, 8, stride=8), :]
                coefficients.append((own + rolled(theirs, dz))[None])
            coefficient = jnp.concatenate(coefficients, 0)
            spins = state[
                1 + dz,
                :,
                target,
                pl.ds(first_x + xi0 + dx, count),
                r0 + shift : r0 + shift + 8,
                :,
            ]
            term = coefficient[None] * spins
            total = term if total is None else total + term
        return total

    def rotate(spin, field):
        w = [TIME_STEP * field[c] for c in range(3)]
        s = [spin[c] for c in range(3)]
        square = w[0] * w[0] + w[1] * w[1] + w[2] * w[2]
        tiny = square < 1e-30
        size = jnp.sqrt(jnp.where(tiny, 1.0, square))
        sine, cosine_half = jnp.sin(0.5 * size), jnp.cos(0.5 * size)
        inverse = 1.0 / size
        half = jnp.where(tiny, 0.5, sine * inverse)
        ratio = 2.0 * half * jnp.where(tiny, 1.0, cosine_half)
        versine = 2.0 * half * half
        turn = 1.0 - versine * jnp.where(tiny, 0.0, square)
        along = versine * (w[0] * s[0] + w[1] * s[1] + w[2] * s[2])
        cross = [
            w[1] * s[2] - w[2] * s[1],
            w[2] * s[0] - w[0] * s[2],
            w[0] * s[1] - w[1] * s[0],
        ]
        return jnp.concatenate(
            [(turn * s[c] + ratio * cross[c] + along * w[c])[None] for c in range(3)], 0
        )

    shape = (3, 2, 8, 128)
    slot_of = lax.broadcasted_iota(jnp.int32, shape, 2)
    z_of = lax.broadcasted_iota(jnp.int32, shape, 3)
    seam = ((z_of >= 64) & (z_of < 66)) | (z_of >= 126)

    def write_targets(sub, first_x, y0, value):
        r0 = 1 + y0
        for dz in (-1, 0, 1):
            state[1 + dz, :, sub, pl.ds(first_x + 1, 2), r0 : r0 + 8, :] = rolled(value, dz)

    def phase(h, y0):
        x0 = 2 * h
        first_x = x0 + 1
        r0 = 1 + y0
        cosines(first_x, 4, y0)
        sides = packed([(62, LOW_SIDE), (126, HIGH_SIDE)])
        results = network([load_cosine(c) for c in MAIN] + [sides])
        for column, value in zip(MAIN, results):
            store_slope(column, value)
        spread(results[-1], LOW_SIDE)
        spread(results[-1], HIGH_SIDE)
        old, trial = [], []
        for sub in (0, 1):
            spin = state[1, :, sub, pl.ds(first_x + 1, 2), r0 : r0 + 8, :]
            old.append(spin)
            trial.append(rotate(spin, fields(sub, 1, 2, first_x, y0)))
        for sub in (0, 1):
            if sub == 0:
                extra = (slot_of == 5) & (z_of == 0)
            else:
                extra = (slot_of == 2) & (z_of == 63)
            change = ((slot_of == 3 + sub) & (z_of < 64)) | extra
            write_targets(sub, first_x, y0, jnp.where(change, trial[sub], old[sub]))
        cosines(first_x, 4, y0)
        groups = (MAIN[:9], MAIN[9:])
        results = network([packed_pair(columns) for columns in groups])
        for columns, value in zip(groups, results):
            spread(value, columns)
        final = []
        for sub in (0, 1):
            spin = state[1, :, sub, pl.ds(first_x + 1, 2), r0 : r0 + 8, :]
            again = rotate(spin, fields(sub, 1, 2, first_x, y0))
            late = (slot_of == 3 + sub) & (z_of >= 64)
            final.append(jnp.where(late, jnp.where(seam, again, trial[sub]), spin))
        for sub in (0, 1):
            write_targets(sub, first_x, y0, final[sub])
            send_buf[h, y0, :, sub, :, :, :] = final[sub][:, :, 3 + sub : 4 + sub, :]

    def copies(h, y0):
        to_yz, to_gx = [], []
        for j, d in enumerate(DELTAS):
            to_yz.append(
                pltpu.make_async_remote_copy(
                    src_ref=send_buf.at[h, y0],
                    dst_ref=got_yz.at[h, y0, j],
                    send_sem=send_sem.at[h, y0, j],
                    recv_sem=recv_yz.at[h, y0, j],
                    device_id=device(0, d),
                    device_id_type=MESH,
                )
            )
        for j, d in enumerate(GX_DELTAS):
            to_gx.append(
                pltpu.make_async_remote_copy(
                    src_ref=send_buf.at[h, y0],
                    dst_ref=got_gx.at[h, y0, j],
                    send_sem=send_sem.at[h, y0, 4 + j],
                    recv_sem=recv_gx.at[h, y0, j],
                    device_id=device(2 * h - 1, d),
                    device_id_type=MESH,
                )
            )
        return to_yz, to_gx

    def take_yz(h, y0):
        for j, d in enumerate(DELTAS):
            y = y0 - 2 * d
            if -4 <= y <= 5:
                put(lambda sub: got_yz[h, y0, j, :, sub], 2 * h + 2, 2, y, 1)

    def take_gx(h, y0):
        for j, d in enumerate(GX_DELTAS):
            put(lambda sub: got_gx[h, y0, j, :, sub], 6 - 6 * h, 2, y0 - 2 * d, 1)

    def half_sweep(h, carry):
        phase(h, 0)
        even_yz, even_gx = copies(h, 0)
        for copy in even_yz + even_gx:
            copy.start()
        for copy in even_yz:
            copy.wait()
        take_yz(h, 0)
        roll_all(2 * h + 2, 2)
        phase(h, 1)
        odd_yz, odd_gx = copies(h, 1)
        for copy in odd_yz + odd_gx:
            copy.start()
        for copy in even_gx + odd_yz + odd_gx:
            copy.wait()
        take_gx(h, 0)
        take_yz(h, 1)
        take_gx(h, 1)
        roll_all(2 * h + 2, 2)
        roll_all(6 - 6 * h, 2)
        return carry

    lax.fori_loop(0, 2, half_sweep, 0)

    for sub in (0, 1):
        spin_out[:, sub] = state[1, :, sub, 2:6, 4 + sub : 6 + sub, :]
    cosines(1, 6, 0)
    results = network([load_cosine(c) for c in FINAL])
    for column, value in zip(FINAL, results):
        store_slope(column, value)
    for sub in (0, 1):
        total = fields(sub, 1, 4, 1, 0)
        field_out[:, sub] = total[:, :, 3 + sub : 5 + sub, :]


def solution(mesh):
    n_gx, n_yz = mesh.shape["gx"], mesh.shape["yz"]

    def per_device(spin, pair, mix, bias, out_w):
        brick = jax.ShapeDtypeStruct(spin.shape, F32)
        vmem = pl.BlockSpec(memory_space=pltpu.VMEM)
        dma = pltpu.SemaphoreType.DMA
        return pl.pallas_call(
            functools.partial(kernel, n_gx, n_yz),
            out_shape=(brick, brick),
            in_specs=[vmem] * 5,
            out_specs=(vmem, vmem),
            scratch_shapes=[
                pltpu.VMEM((3, 3, 2, 8, 16, 128), F32),
                pltpu.VMEM((2 * NT * 8, 128), F32),
                pltpu.VMEM(((2 * NT + 2) * 8, 128), F32),
                pltpu.VMEM((256, 256), BF16),
                pltpu.VMEM((256, 256), BF16),
                pltpu.VMEM((128, 128), F32),
                pltpu.VMEM((4, 3, 2, 4, 2, 128), F32),
                pltpu.VMEM((5, 3, 2, 2, 2, 128), F32),
                pltpu.VMEM((2, 2, 3, 2, 2, 1, 128), F32),
                pltpu.VMEM((2, 2, 4, 3, 2, 2, 1, 128), F32),
                pltpu.VMEM((2, 2, 5, 3, 2, 2, 1, 128), F32),
                dma((9,)),
                dma((9,)),
                dma((2, 2, 9)),
                dma((2, 2, 4)),
                dma((2, 2, 5)),
            ],
            compiler_params=pltpu.CompilerParams(collective_id=0, has_side_effects=True),
        )(spin, pair, mix, bias.reshape(1, 128), out_w.reshape(1, 128))

    placed = (P(None, None, "gx", "yz", None), P(), P(), P(), P())
    return jax.shard_map(
        per_device,
        mesh=mesh,
        in_specs=placed,
        out_specs=(P(None, None, "gx", "yz", None), P(None, None, "gx", "yz", None)),
        check_vma=False,
    )
```

profile of v0, /device:TPU:1, one launch (start us, length us, event | category | flops | bytes accessed | tf_op | source)
XLA Modules:
  0.0 56.0 jit_solution(13483236998647078405)
XLA Ops:
  0.6 53.4 %shard_map.68 = (f32[3,2,4,2,128]{4,3,2,1,0:T(2,128)}, f32[3,2,4,2,128]{4,3,2,1,0:T(2,128)}) custom-call(f32[3,2,4,2,128]{4,3,2,1,0:T(2,128)} %spin_ref.1, f32[112,128]{1,0:T(8,128)} %pair_ref.1, f32[128,128]{1,0:T(8,128)} %mix_ref.1, f32[1,128]{1,0:T(1,128)} %bitcast.2, f32[1,128]{1,0:T(1,128)} %bitcast.3), custom_call_target="tpu_custom_call" | custom-call | tf_op jit(solution)/shard_map/pallas_call | solution.py:453
  54.1 0.0 copy-start
  54.1 1.4 %copy.9 = f32[3,2,4,2,128]{4,3,2,1,0:T(2,128)} copy(f32[3,2,4,2,128]{4,3,2,1,0:T(2,128)} %get-tuple-element.4) | data formatting | bytes 49152
  55.4 0.0 copy-done
  55.4 0.6 %copy.10 = f32[3,2,4,2,128]{4,3,2,1,0:T(2,128)} copy(f32[3,2,4,2,128]{4,3,2,1,0:T(2,128)S(1)} %copy-done) | data formatting | bytes 49152
Async XLA Ops:
  54.1 1.4 %copy-start = (f32[3,2,4,2,128]{4,3,2,1,0:T(2,128)S(1)}, f32[3,2,4,2,128]{4,3,2,1,0:T(2,128)}, u32[]{:S(2)}) copy-start(f32[3,2,4,2,128]{4,3,2,1,0:T(2,128)} %get-tuple-element.5) | copy-start | bytes 73732
where the time goes:
time: 56.2 us; the launch traced here: 56 us
  Pallas kernels  53.4 us (95%)
  local copies, waits for them, and re-layouts  1.96 us (3%)
  between operations  0.65 us (1%)
    pallas_call x1, Pallas kernels, per_device(): pl.pallas_call(functools.partial(kernel, n_gx, n_yz), out_shape=(brick, b...  53.4 us
    unnamed x4, local copies, waits for them, and re-layouts  1.96 us

commit v1 on v0

--- a/solution.py
+++ b/solution.py
@@ -12,7 +12,7 @@
 NXI = 6
 NT = 2 * NXI * 8
 TIME_STEP = 0.1
-CHUNK = 4
+CHUNK = 2
 F32 = jnp.float32
 BF16 = jnp.bfloat16
 
@@ -52,13 +52,49 @@
 
 
 MAIN = columns_of(with_neighbours([(s, x, 0, 0) for s in (0, 1) for x in (0, 1)]))
-LOW_SIDE = columns_of(with_neighbours([(1, x, -2, 63) for x in (0, 1)]))
-HIGH_SIDE = columns_of(with_neighbours([(0, x, 2, 0) for x in (0, 1)]))
-LOW_SIDE = [c for c in LOW_SIDE if c not in MAIN]
-HIGH_SIDE = [c for c in HIGH_SIDE if c not in MAIN]
-FINAL = columns_of(
-    with_neighbours([(s, x, y, 0) for s in (0, 1) for x in range(4) for y in (0, 1)])
-)
+LOW_SEED = [(1, x, -2, 63) for x in (0, 1)]
+HIGH_SEED = [(0, x, 2, 0) for x in (0, 1)]
+LOW_SIDE = [c for c in columns_of(with_neighbours(LOW_SEED)) if c not in MAIN]
+HIGH_SIDE = [c for c in columns_of(with_neighbours(HIGH_SEED)) if c not in MAIN]
+OWN = [(s, x, y, 0) for s in (0, 1) for x in range(4) for y in (0, 1)]
+FINAL = columns_of(with_neighbours(OWN))
+
+
+def places_of(atoms):
+    return {(a[1], a[2]) for a in with_neighbours(with_neighbours(atoms))}
+
+
+def phase_reads(h, y0):
+    seeds = [(s, x, 0, z) for s in (0, 1) for x in (0, 1) for z in (0, 64)]
+    places = places_of(seeds + LOW_SEED + HIGH_SEED)
+    return {(x + 2 * h, y + y0) for x, y in places}
+
+
+FINAL_READS = places_of(OWN)
+
+
+def message_places(h, y0, dgx, e):
+    return {(4 * dgx + 2 * h + x, y0 + 2 * e) for x in (0, 1)}
+
+
+def sources(h, y0):
+    later = [(h, y0, phase_reads(h, y0)) for h, y0 in PHASES[2 * h + y0 + 1 :]]
+    later.append((2, 0, FINAL_READS))
+    result = {}
+    for dgx in (0, 1, -1):
+        for e in (0, 1, -1, 2, -2):
+            if (dgx, e) == (0, 0):
+                continue
+            for rank, (_, _, reads) in enumerate(later):
+                if message_places(h, y0, dgx, e) & reads:
+                    result[(dgx, e)] = 2 * h + y0 + 1 + rank
+                    break
+    return result
+
+
+PHASES = [(0, 0), (0, 1), (1, 0), (1, 1)]
+SOURCES = [sources(h, y0) for h, y0 in PHASES]
+ORDERED = [sorted(found, key=lambda d: (found[d], d)) for found in SOURCES]
 
 
 def tile(sub, xi, slot, half):
@@ -93,13 +129,11 @@
     start_yz,
     start_gx,
     send_buf,
-    got_yz,
-    got_gx,
+    got,
     start_send,
     start_recv,
     send_sem,
-    recv_yz,
-    recv_gx,
+    recv_sem,
 ):
     gx = lax.axis_index("gx")
     yz = lax.axis_index("yz")
@@ -171,13 +205,13 @@
     def put(value_of_sub, first_x, count, y, rows):
         for sub in (0, 1):
             r = y + 4 + sub
-            state[1, :, sub, pl.ds(first_x, count), r : r + rows, :] = value_of_sub(sub)
+            state[1, :, sub, first_x : first_x + count, r : r + rows, :] = value_of_sub(sub)
 
     def roll_all(first_x, count):
         for sub in (0, 1):
-            value = state[1, :, sub, pl.ds(first_x, count), :, :]
-            state[0, :, sub, pl.ds(first_x, count), :, :] = rolled(value, -1)
-            state[2, :, sub, pl.ds(first_x, count), :, :] = rolled(value, 1)
+            value = state[1, :, sub, first_x : first_x + count]
+            state[0, :, sub, first_x : first_x + count] = rolled(value, -1)
+            state[2, :, sub, first_x : first_x + count] = rolled(value, 1)
 
     put(lambda sub: spin_ref[:, sub], 2, 4, 0, 2)
     for copy in starts:
@@ -188,23 +222,38 @@
         put(lambda sub: start_gx[j, :, sub], 0, 2, -2 * d, 2)
     roll_all(0, 6)
 
-    def cosines(first_x, count, y0):
+    def cosines(first_x, y0, groups, touched=None):
         r0 = 1 + y0
-        for sub in (0, 1):
-            centre = state[1, :, sub, pl.ds(first_x, count), r0 : r0 + 8, :]
-            for o, (target, dx, dy, dz) in enumerate(BONDS[sub]):
-                r = r0 + row_shift(sub, target, dy)
-                other = state[1 + dz, :, target, pl.ds(first_x + dx, count), r : r + 8, :]
+        for sub, bonds in ((0, (0, 1, 2, 3, 4, 5, 6, 7, 8, 10, 12)), (1, (8, 10, 12))):
+            for o in bonds:
+                target, dx, dy, dz = BONDS[sub][o]
+                mate = partner(o)
+                shift = row_shift(sub, target, dy)
+                wanted = [
+                    xi
+                    for xi in range(-1, NXI + 1)
+                    if ((sub, xi) in groups or (target, xi + dx) in groups)
+                    and (touched is None or xi in touched or xi + dx in touched)
+                ]
+                first, count = wanted[0], wanted[-1] - wanted[0] + 1
+                centre = state[1, :, sub, first_x + first : first_x + first + count, r0 : r0 + 8]
+                r, x = r0 + shift, first_x + first + dx
+                other = state[1 + dz, :, target, x : x + count, r : r + 8]
                 product = centre * other
                 value = product[0] + product[1] + product[2]
-                for xi in range(count):
-                    at = tile(sub, xi, 0, o // 8) * 8 + o % 8
-                    cosine[pl.ds(at, 8, stride=8), :] = value[xi]
+                back = rolled(value, -dz)
+                for xi in wanted:
+                    if (sub, xi) in groups:
+                        at = (tile(sub, xi, 0, o // 8) + 1) * 8 + o % 8
+                        cosine[pl.ds(at, 8, stride=8), :] = value[xi - first]
+                    if (target, xi + dx) in groups:
+                        at = (tile(target, xi + dx, shift, mate // 8) + 1) * 8 + mate % 8
+                        cosine[pl.ds(at, 8, stride=8), :] = back[xi - first]
 
     def load_cosine(column):
         halves = []
         for half in (0, 1):
-            at = column_tile(column, half) * 8
+            at = column_tile(column, half) * 8 + 8
             halves.append(cosine[at : at + 8, :])
         return jnp.concatenate(halves, 0)
 
@@ -294,7 +343,7 @@
                 1 + dz,
                 :,
                 target,
-                pl.ds(first_x + xi0 + dx, count),
+                first_x + xi0 + dx : first_x + xi0 + dx + count,
                 r0 + shift : r0 + shift + 8,
                 :,
             ]
@@ -332,22 +381,62 @@
     def write_targets(sub, first_x, y0, value):
         r0 = 1 + y0
         for dz in (-1, 0, 1):
-            state[1 + dz, :, sub, pl.ds(first_x + 1, 2), r0 : r0 + 8, :] = rolled(value, dz)
+            state[1 + dz, :, sub, first_x + 1 : first_x + 3, r0 : r0 + 8, :] = rolled(value, dz)
+
+    def evaluate(columns):
+        for column, value in zip(columns, network([load_cosine(c) for c in columns])):
+            store_slope(column, value)
+
+    def groups_of(columns):
+        return {(c[0], c[1] + 1) for c in columns}
+
+    def split(columns, arriving, origin):
+        early, late = [], []
+        for sub, x, y in columns:
+            around = {(a[1] + origin[0], a[2] + origin[1]) for a in with_neighbours([(sub, x, y, 0)])}
+            (late if around & arriving else early).append((sub, x, y))
+        return early, late
+
+    def gather(columns, first_x, y0, origin, reader):
+        groups = groups_of(columns + (LOW_SIDE + HIGH_SIDE if reader < 4 else []))
+        if reader == 0:
+            cosines(first_x, y0, groups)
+            return columns
+        arriving = set()
+        for p in range(reader):
+            for source in ORDERED[p]:
+                if SOURCES[p][source] == reader:
+                    if p < reader - 1:
+                        receive(p, source)
+                    else:
+                        arriving |= message_places(*PHASES[p], *source)
+        for p in range(reader - 1):
+            reroll(p, reader)
+        early, late = split(columns, arriving, origin)
+        cosines(first_x, y0, groups)
+        evaluate(early)
+        for source in ORDERED[reader - 1]:
+            if SOURCES[reader - 1][source] == reader:
+                receive(reader - 1, source)
+        reroll(reader - 1, reader)
+        touched = {x + 2 - first_x for x, _ in arriving}
+        cosines(first_x, y0, groups, touched)
+        return late
 
     def phase(h, y0):
         x0 = 2 * h
         first_x = x0 + 1
         r0 = 1 + y0
-        cosines(first_x, 4, y0)
+        late = gather(MAIN, first_x, y0, (x0, y0), 2 * h + y0)
         sides = packed([(62, LOW_SIDE), (126, HIGH_SIDE)])
-        results = network([load_cosine(c) for c in MAIN] + [sides])
-        for column, value in zip(MAIN, results):
+        results = network([load_cosine(c) for c in late] + [sides])
+        for column, value in zip(late, results):
             store_slope(column, value)
         spread(results[-1], LOW_SIDE)
         spread(results[-1], HIGH_SIDE)
         old, trial = [], []
         for sub in (0, 1):
-            spin = state[1, :, sub, pl.ds(first_x + 1, 2), r0 : r0 + 8, :]
+            spin = state[1, :, sub, first_x + 1 : first_x + 3, r0 : r0 + 8, :]
             old.append(spin)
             trial.append(rotate(spin, fields(sub, 1, 2, first_x, y0)))
         for sub in (0, 1):
@@ -357,87 +446,56 @@
                 extra = (slot_of == 2) & (z_of == 63)
             change = ((slot_of == 3 + sub) & (z_of < 64)) | extra
             write_targets(sub, first_x, y0, jnp.where(change, trial[sub], old[sub]))
-        cosines(first_x, 4, y0)
+        cosines(first_x, y0, groups_of(MAIN), {1, 2})
         groups = (MAIN[:9], MAIN[9:])
         results = network([packed_pair(columns) for columns in groups])
         for columns, value in zip(groups, results):
             spread(value, columns)
         final = []
         for sub in (0, 1):
-            spin = state[1, :, sub, pl.ds(first_x + 1, 2), r0 : r0 + 8, :]
+            spin = state[1, :, sub, first_x + 1 : first_x + 3, r0 : r0 + 8, :]
             again = rotate(spin, fields(sub, 1, 2, first_x, y0))
             late = (slot_of == 3 + sub) & (z_of >= 64)
             final.append(jnp.where(late, jnp.where(seam, again, trial[sub]), spin))
         for sub in (0, 1):
             write_targets(sub, first_x, y0, final[sub])
-            send_buf[h, y0, :, sub, :, :, :] = final[sub][:, :, 3 + sub : 4 + sub, :]
-
-    def copies(h, y0):
-        to_yz, to_gx = [], []
-        for j, d in enumerate(DELTAS):
-            to_yz.append(
-                pltpu.make_async_remote_copy(
-                    src_ref=send_buf.at[h, y0],
-                    dst_ref=got_yz.at[h, y0, j],
-                    send_sem=send_sem.at[h, y0, j],
-                    recv_sem=recv_yz.at[h, y0, j],
-                    device_id=device(0, d),
-                    device_id_type=MESH,
-                )
+            send_buf[2 * h + y0, :, sub, :, :, :] = final[sub][:, :, 3 + sub : 4 + sub, :]
+
+    started = {}
+
+    def send(p):
+        for j, (dgx, e) in enumerate(ORDERED[p]):
+            copy = pltpu.make_async_remote_copy(
+                src_ref=send_buf.at[p],
+                dst_ref=got.at[p, j],
+                send_sem=send_sem.at[p, j],
+                recv_sem=recv_sem.at[p, j],
+                device_id=device(-dgx, -e),
+                device_id_type=MESH,
             )
-        for j, d in enumerate(GX_DELTAS):
-            to_gx.append(
-                pltpu.make_async_remote_copy(
-                    src_ref=send_buf.at[h, y0],
-                    dst_ref=got_gx.at[h, y0, j],
-                    send_sem=send_sem.at[h, y0, 4 + j],
-                    recv_sem=recv_gx.at[h, y0, j],
-                    device_id=device(2 * h - 1, d),
-                    device_id_type=MESH,
-                )
-            )
-        return to_yz, to_gx
-
-    def take_yz(h, y0):
-        for j, d in enumerate(DELTAS):
-            y = y0 - 2 * d
-            if -4 <= y <= 5:
-                put(lambda sub: got_yz[h, y0, j, :, sub], 2 * h + 2, 2, y, 1)
-
-    def take_gx(h, y0):
-        for j, d in enumerate(GX_DELTAS):
-            put(lambda sub: got_gx[h, y0, j, :, sub], 6 - 6 * h, 2, y0 - 2 * d, 1)
-
-    def half_sweep(h, carry):
-        phase(h, 0)
-        even_yz, even_gx = copies(h, 0)
-        for copy in even_yz + even_gx:
             copy.start()
-        for copy in even_yz:
-            copy.wait()
-        take_yz(h, 0)
-        roll_all(2 * h + 2, 2)
-        phase(h, 1)
-        odd_yz, odd_gx = copies(h, 1)
-        for copy in odd_yz + odd_gx:
-            copy.start()
-        for copy in even_gx + odd_yz + odd_gx:
-            copy.wait()
-        take_gx(h, 0)
-        take_yz(h, 1)
-        take_gx(h, 1)
-        roll_all(2 * h + 2, 2)
-        roll_all(6 - 6 * h, 2)
-        return carry
-
-    lax.fori_loop(0, 2, half_sweep, 0)
+            started[(p, (dgx, e))] = copy
+
+    def receive(p, source):
+        started[(p, source)].wait()
+        h, y0 = PHASES[p]
+        j = ORDERED[p].index(source)
+        dgx, e = source
+        put(lambda sub: got[p, j, :, sub], 4 * dgx + 2 * h + 2, 2, y0 + 2 * e, 1)
+
+    def reroll(p, reader):
+        h, _ = PHASES[p]
+        for dgx in (0, 1, -1):
+            if any(d[0] == dgx and SOURCES[p][d] == reader for d in ORDERED[p]):
+                roll_all(4 * dgx + 2 * h + 2, 2)
+
+    for p in range(4):
+        phase(*PHASES[p])
+        send(p)
 
     for sub in (0, 1):
         spin_out[:, sub] = state[1, :, sub, 2:6, 4 + sub : 6 + sub, :]
-    cosines(1, 6, 0)
-    results = network([load_cosine(c) for c in FINAL])
-    for column, value in zip(FINAL, results):
-        store_slope(column, value)
+    evaluate(gather(FINAL, 1, 0, (0, 0), 4))
     for sub in (0, 1):
         total = fields(sub, 1, 4, 1, 0)
         field_out[:, sub] = total[:, :, 3 + sub : 5 + sub, :]
@@ -457,21 +515,19 @@
             out_specs=(vmem, vmem),
             scratch_shapes=[
                 pltpu.VMEM((3, 3, 2, 8, 16, 128), F32),
-                pltpu.VMEM((2 * NT * 8, 128), F32),
+                pltpu.VMEM(((2 * NT + 2) * 8, 128), F32),
                 pltpu.VMEM(((2 * NT + 2) * 8, 128), F32),
                 pltpu.VMEM((256, 256), BF16),
                 pltpu.VMEM((256, 256), BF16),
                 pltpu.VMEM((128, 128), F32),
                 pltpu.VMEM((4, 3, 2, 4, 2, 128), F32),
                 pltpu.VMEM((5, 3, 2, 2, 2, 128), F32),
-                pltpu.VMEM((2, 2, 3, 2, 2, 1, 128), F32),
-                pltpu.VMEM((2, 2, 4, 3, 2, 2, 1, 128), F32),
-                pltpu.VMEM((2, 2, 5, 3, 2, 2, 1, 128), F32),
+                pltpu.VMEM((4, 3, 2, 2, 1, 128), F32),
+                pltpu.VMEM((4, 9, 3, 2, 2, 1, 128), F32),
                 dma((9,)),
                 dma((9,)),
-                dma((2, 2, 9)),
-                dma((2, 2, 4)),
-                dma((2, 2, 5)),
+                dma((4, 9)),
+                dma((4, 9)),
             ],
             compiler_params=pltpu.CompilerParams(collective_id=0, has_side_effects=True),
         )(spin, pair, mix, bias.reshape(1, 128), out_w.reshape(1, 128))

time: 56.2 us -> 49 us (0.87)
  Pallas kernels: 53.4 us -> 46.2 us
    pallas_call x1, Pallas kernels: 53.4 us -> 46.2 us  [per_device(): pl.pallas_call(functools.partial(kernel, n_gx, n_yz), out_shape=(brick, b...]
where the time goes in v1:
time: 49 us; the launch traced here: 48.8 us
  Pallas kernels  46.2 us (94%)
  local copies, waits for them, and re-layouts  1.96 us (4%)
  between operations  0.65 us (1%)
    pallas_call x1, Pallas kernels, per_device(): pl.pallas_call(functools.partial(kernel, n_gx, n_yz), out_shape=(brick, b...  46.2 us
    unnamed x4, local copies, waits for them, and re-layouts  1.96 us

profile of v1, /device:TPU:1, one launch (start us, length us, event | category | flops | bytes accessed | tf_op | source)
XLA Modules:
  0.0 48.8 jit_solution(15414066501926046335)
XLA Ops:
  0.6 46.2 %shard_map.68 = (f32[3,2,4,2,128]{4,3,2,1,0:T(2,128)}, f32[3,2,4,2,128]{4,3,2,1,0:T(2,128)}) custom-call(f32[3,2,4,2,128]{4,3,2,1,0:T(2,128)} %spin_ref.1, f32[112,128]{1,0:T(8,128)} %pair_ref.1, f32[128,128]{1,0:T(8,128)} %mix_ref.1, f32[1,128]{1,0:T(1,128)} %bitcast.2, f32[1,128]{1,0:T(1,128)} %bitcast.3), custom_call_target="tpu_custom_call" | custom-call | tf_op jit(solution)/shard_map/pallas_call | solution.py:511
  46.9 0.0 copy-start
  46.9 1.4 %copy.9 = f32[3,2,4,2,128]{4,3,2,1,0:T(2,128)} copy(f32[3,2,4,2,128]{4,3,2,1,0:T(2,128)} %get-tuple-element.4) | data formatting | bytes 49152
  48.2 0.0 copy-done
  48.2 0.6 %copy.10 = f32[3,2,4,2,128]{4,3,2,1,0:T(2,128)} copy(f32[3,2,4,2,128]{4,3,2,1,0:T(2,128)S(1)} %copy-done) | data formatting | bytes 49152
Async XLA Ops:
  46.9 1.4 %copy-start = (f32[3,2,4,2,128]{4,3,2,1,0:T(2,128)S(1)}, f32[3,2,4,2,128]{4,3,2,1,0:T(2,128)}, u32[]{:S(2)}) copy-start(f32[3,2,4,2,128]{4,3,2,1,0:T(2,128)} %get-tuple-element.5) | copy-start | bytes 73732

commit v2 on v1

--- a/solution.py
+++ b/solution.py
@@ -1,4 +1,5 @@
 import functools
+import math
 
 import jax
 import jax.numpy as jnp
@@ -10,7 +11,6 @@
 MESH = pl.DeviceIdType.MESH
 NB = 8
 NXI = 6
-NT = 2 * NXI * 8
 TIME_STEP = 0.1
 CHUNK = 2
 F32 = jnp.float32
@@ -97,13 +97,35 @@
 ORDERED = [sorted(found, key=lambda d: (found[d], d)) for found in SOURCES]
 
 
-def tile(sub, xi, slot, half):
-    return half * NT + (sub * NXI + xi) * 8 + slot
-
-
-def column_tile(column, half):
-    sub, x, y = column
-    return tile(sub, x + 1, y + 3 + sub, half)
+def sine_cosine(x):
+    n = jnp.floor(x * (2.0 / math.pi) + 0.5)
+    y = ((x - n * 1.5703125) - n * 4.83751296997e-4) - n * 7.54978995489e-8
+    y2 = y * y
+    sine = y + y * y2 * (-1.6666654611e-1 + y2 * (8.3321608736e-3 - y2 * 1.9515295891e-4))
+    cosine = 1.0 - 0.5 * y2 + y2 * y2 * (
+        4.166664568298827e-2 + y2 * (-1.388731625493765e-3 + y2 * 2.443315711809948e-5)
+    )
+    quarter = n - 4.0 * jnp.floor(0.25 * n)
+    odd = (quarter == 1.0) | (quarter == 3.0)
+    first, second = jnp.where(odd, cosine, sine), jnp.where(odd, sine, cosine)
+    first = jnp.where(quarter >= 2.0, -first, first)
+    second = jnp.where((quarter == 1.0) | (quarter == 2.0), -second, second)
+    return first, second
+
+
+def exchange(rows):
+    shape = rows[0].shape
+    place = lax.broadcasted_iota(jnp.int32, shape, 1)
+    rows = list(rows)
+    for step in (4, 2, 1):
+        low = (place & step) == 0
+        for i in range(8):
+            if i & step:
+                continue
+            a, b = rows[i], rows[i + step]
+            rows[i] = jnp.where(low, a, pltpu.roll(b, step, 1))
+            rows[i + step] = jnp.where(low, pltpu.roll(a, 8 - step, 1), b)
+    return rows
 
 
 def rolled(value, dz):
@@ -113,19 +135,25 @@
 def kernel(
     n_gx,
     n_yz,
+    spin_hbm,
+    pair_hbm,
+    mix_hbm,
+    bias_hbm,
+    out_w_hbm,
+    both_out,
+    state,
+    cosine,
+    slope,
+    by_bond,
+    first_w,
+    second_w,
+    scratch_w,
     spin_ref,
     pair_ref,
     mix_ref,
     bias_ref,
     out_w_ref,
-    spin_out,
-    field_out,
-    state,
-    cosine,
-    slope,
-    first_w,
-    second_w,
-    scratch_w,
+    load_sem,
     start_yz,
     start_gx,
     send_buf,
@@ -146,6 +174,52 @@
     for dgx, dyz in partners:
         pl.semaphore_signal(barrier, inc=1, device_id=device(dgx, dyz), device_id_type=MESH)
 
+    loads = []
+    for j, (source, target) in enumerate(
+        (
+            (spin_hbm, spin_ref),
+            (pair_hbm, pair_ref),
+            (mix_hbm, mix_ref),
+            (bias_hbm, bias_ref),
+            (out_w_hbm, out_w_ref),
+        )
+    ):
+        load = pltpu.make_async_copy(source, target, load_sem.at[j])
+        load.start()
+        loads.append(load)
+    slope[...] = jnp.zeros(slope.shape, F32)
+    state[...] = jnp.zeros(state.shape, F32)
+
+    pl.semaphore_wait(barrier, len(partners))
+
+    starts = []
+    for j, d in enumerate(DELTAS):
+        starts.append(
+            pltpu.make_async_remote_copy(
+                src_ref=spin_hbm,
+                dst_ref=start_yz.at[j],
+                send_sem=start_send.at[j],
+                recv_sem=start_recv.at[j],
+                device_id=device(0, d),
+                device_id_type=MESH,
+            )
+        )
+    for j, d in enumerate(GX_DELTAS):
+        starts.append(
+            pltpu.make_async_remote_copy(
+                src_ref=spin_hbm.at[:, :, 2:4],
+                dst_ref=start_gx.at[j],
+                send_sem=start_send.at[4 + j],
+                recv_sem=start_recv.at[4 + j],
+                device_id=device(1, d),
+                device_id_type=MESH,
+            )
+        )
+    for copy in starts:
+        copy.start()
+
+    for load in loads:
+        load.wait()
     scratch_w[...] = jnp.zeros((128, 128), F32)
     for k in range(NB):
         scratch_w[16 * k : 16 * k + 8, :] = pair_ref[pl.ds(k, 8, stride=8), :]
@@ -168,40 +242,8 @@
             [jnp.concatenate([high, high], 1), jnp.concatenate([low, low], 1)], 0
         )
 
-    first_w[...] = stacked(with_bias.T)
+    first_w[...] = stacked(0.5 * with_bias.T)
     second_w[...] = stacked(scaled)
-    cosine[...] = jnp.ones(cosine.shape, F32)
-    slope[...] = jnp.zeros(slope.shape, F32)
-    state[...] = jnp.zeros(state.shape, F32)
-
-    pl.semaphore_wait(barrier, len(partners))
-
-    starts = []
-    for j, d in enumerate(DELTAS):
-        starts.append(
-            pltpu.make_async_remote_copy(
-                src_ref=spin_ref,
-                dst_ref=start_yz.at[j],
-                send_sem=start_send.at[j],
-                recv_sem=start_recv.at[j],
-                device_id=device(0, d),
-                device_id_type=MESH,
-            )
-        )
-    for j, d in enumerate(GX_DELTAS):
-        starts.append(
-            pltpu.make_async_remote_copy(
-                src_ref=spin_ref.at[:, :, 2:4],
-                dst_ref=start_gx.at[j],
-                send_sem=start_send.at[4 + j],
-                recv_sem=start_recv.at[4 + j],
-                device_id=device(1, d),
-                device_id_type=MESH,
-            )
-        )
-    for copy in starts:
-        copy.start()
-
     def put(value_of_sub, first_x, count, y, rows):
         for sub in (0, 1):
             r = y + 4 + sub
@@ -222,45 +264,38 @@
         put(lambda sub: start_gx[j, :, sub], 0, 2, -2 * d, 2)
     roll_all(0, 6)
 
-    def cosines(first_x, y0, groups, touched=None):
+    def cosines(first_x, y0, count):
         r0 = 1 + y0
-        for sub, bonds in ((0, (0, 1, 2, 3, 4, 5, 6, 7, 8, 10, 12)), (1, (8, 10, 12))):
-            for o in bonds:
-                target, dx, dy, dz = BONDS[sub][o]
-                mate = partner(o)
-                shift = row_shift(sub, target, dy)
-                wanted = [
-                    xi
-                    for xi in range(-1, NXI + 1)
-                    if ((sub, xi) in groups or (target, xi + dx) in groups)
-                    and (touched is None or xi in touched or xi + dx in touched)
-                ]
-                first, count = wanted[0], wanted[-1] - wanted[0] + 1
-                centre = state[1, :, sub, first_x + first : first_x + first + count, r0 : r0 + 8]
-                r, x = r0 + shift, first_x + first + dx
-                other = state[1 + dz, :, target, x : x + count, r : r + 8]
-                product = centre * other
-                value = product[0] + product[1] + product[2]
-                back = rolled(value, -dz)
-                for xi in wanted:
-                    if (sub, xi) in groups:
-                        at = (tile(sub, xi, 0, o // 8) + 1) * 8 + o % 8
-                        cosine[pl.ds(at, 8, stride=8), :] = value[xi - first]
-                    if (target, xi + dx) in groups:
-                        at = (tile(target, xi + dx, shift, mate // 8) + 1) * 8 + mate % 8
-                        cosine[pl.ds(at, 8, stride=8), :] = back[xi - first]
+        for sub in (0, 1):
+            centre = state[1, :, sub, first_x : first_x + count, r0 : r0 + 8]
+            for half in (0, 1):
+                values = []
+                for target, dx, dy, dz in BONDS[sub][8 * half : 8 * half + 8]:
+                    r, x = r0 + row_shift(sub, target, dy), first_x + dx
+                    product = centre * state[1 + dz, :, target, x : x + count, r : r + 8]
+                    values.append(product[0] + product[1] + product[2])
+                values += [jnp.ones((count, 8, 128), F32)] * (8 - len(values))
+                for slot, value in enumerate(exchange(values)):
+                    if 1 <= slot <= 6:
+                        cosine[half, sub, 0:count, slot] = value
 
     def load_cosine(column):
-        halves = []
+        sub, x, y = column
+        return jnp.concatenate([cosine[half, sub, x + 1, y + 3 + sub] for half in (0, 1)], 0)
+
+    def store_slope(column, value):
+        sub, x, y = column
         for half in (0, 1):
-            at = column_tile(column, half) * 8 + 8
-            halves.append(cosine[at : at + 8, :])
-        return jnp.concatenate(halves, 0)
-
-    def store_slope(column, value):
-        for half in (0, 1):
-            at = column_tile(column, half) * 8 + 8
-            slope[at : at + 8, :] = value[8 * half : 8 * half + 8, :]
+            slope[half, sub, x + 1, y + 3 + sub] = value[8 * half : 8 * half + 8, :]
+
+    def slopes_by_bond(count):
+        for sub in (0, 1):
+            for half in (0, 1):
+                zero = jnp.zeros((count, 8, 128), F32)
+                values = [zero] + [slope[half, sub, 0:count, slot] for slot in range(1, 7)] + [zero]
+                for o, value in enumerate(exchange(values)):
+                    if 8 * half + o < 14:
+                        by_bond[sub, 8 * half + o, 0:count, 8:16, :] = value
 
     def product(weight, value):
         high = value.astype(BF16)
@@ -276,11 +311,12 @@
             part = values[begin : begin + CHUNK]
             c = jnp.concatenate(part, 1)
             twice = c + c
-            firsts = [jnp.ones_like(c), c]
-            seconds = [jnp.ones_like(c), twice]
-            for _ in range(2, NB + 1):
+            firsts = [None, twice, twice * twice - 2.0]
+            for _ in range(3, NB + 1):
                 firsts.append(twice * firsts[-1] - firsts[-2])
-                seconds.append(twice * seconds[-1] - seconds[-2])
+            seconds = [None, twice, firsts[2] + 1.0]
+            for k in range(3, NB):
+                seconds.append(firsts[k] + seconds[k - 2])
             u = jnp.tanh(product(first_w, jnp.concatenate(firsts[1:], 0)))
             d = product(second_w, 1.0 - u * u)
             g = d[0:16]
@@ -294,7 +330,7 @@
     def packed(groups):
         result = None
         for first, columns in groups:
-            order = lax.rem(lane + (256 - first), 128)
+            order = (lane + (256 - first)) & 127
             for m, column in enumerate(columns):
                 value = load_cosine(column)
                 if m:
@@ -308,8 +344,8 @@
 
     def packed_pair(columns):
         result = None
-        low = lax.rem(lane + (256 - 63), 128)
-        high = lax.rem(lane + (256 - 125), 128)
+        low = (lane + (256 - 63)) & 127
+        high = (lane + (256 - 125)) & 127
         for m, column in enumerate(columns):
             value = load_cosine(column)
             if m:
@@ -329,16 +365,11 @@
         r0 = 1 + y0
         total = None
         for o, (target, dx, dy, dz) in enumerate(BONDS[sub]):
-            mate = partner(o)
             shift = row_shift(sub, target, dy)
-            coefficients = []
-            for xi in range(xi0, xi0 + count):
-                at = (tile(sub, xi, 0, o // 8) + 1) * 8 + o % 8
-                own = slope[pl.ds(at, 8, stride=8), :]
-                at = (tile(target, xi + dx, shift, mate // 8) + 1) * 8 + mate % 8
-                theirs = slope[pl.ds(at, 8, stride=8), :]
-                coefficients.append((own + rolled(theirs, dz))[None])
-            coefficient = jnp.concatenate(coefficients, 0)
+            own = by_bond[sub, o, xi0 : xi0 + count, 8:16, :]
+            r, xi = 8 + shift, xi0 + dx
+            theirs = by_bond[target, partner(o), xi : xi + count, r : r + 8, :]
+            coefficient = own + rolled(theirs, dz)
             spins = state[
                 1 + dz,
                 :,
@@ -357,7 +388,7 @@
         square = w[0] * w[0] + w[1] * w[1] + w[2] * w[2]
         tiny = square < 1e-30
         size = jnp.sqrt(jnp.where(tiny, 1.0, square))
-        sine, cosine_half = jnp.sin(0.5 * size), jnp.cos(0.5 * size)
+        sine, cosine_half = sine_cosine(0.5 * size)
         inverse = 1.0 / size
         half = jnp.where(tiny, 0.5, sine * inverse)
         ratio = 2.0 * half * jnp.where(tiny, 1.0, cosine_half)
@@ -387,9 +418,6 @@
         for column, value in zip(columns, network([load_cosine(c) for c in columns])):
             store_slope(column, value)
 
-    def groups_of(columns):
-        return {(c[0], c[1] + 1) for c in columns}
-
     def split(columns, arriving, origin):
         early, late = [], []
         for sub, x, y in columns:
@@ -398,9 +426,9 @@
         return early, late
 
     def gather(columns, first_x, y0, origin, reader):
-        groups = groups_of(columns + (LOW_SIDE + HIGH_SIDE if reader < 4 else []))
+        count = 4 if reader < 4 else NXI
         if reader == 0:
-            cosines(first_x, y0, groups)
+            cosines(first_x, y0, count)
             return columns
         arriving = set()
         for p in range(reader):
@@ -413,14 +441,13 @@
         for p in range(reader - 1):
             reroll(p, reader)
         early, late = split(columns, arriving, origin)
-        cosines(first_x, y0, groups)
+        cosines(first_x, y0, count)
         evaluate(early)
         for source in ORDERED[reader - 1]:
             if SOURCES[reader - 1][source] == reader:
                 receive(reader - 1, source)
         reroll(reader - 1, reader)
-        touched = {x + 2 - first_x for x, _ in arriving}
-        cosines(first_x, y0, groups, touched)
+        cosines(first_x, y0, count)
         return late
 
     def phase(h, y0):
@@ -434,6 +461,7 @@
             store_slope(column, value)
         spread(results[-1], LOW_SIDE)
         spread(results[-1], HIGH_SIDE)
+        slopes_by_bond(4)
         old, trial = [], []
         for sub in (0, 1):
             spin = state[1, :, sub, first_x + 1 : first_x + 3, r0 : r0 + 8, :]
@@ -446,11 +474,12 @@
                 extra = (slot_of == 2) & (z_of == 63)
             change = ((slot_of == 3 + sub) & (z_of < 64)) | extra
             write_targets(sub, first_x, y0, jnp.where(change, trial[sub], old[sub]))
-        cosines(first_x, y0, groups_of(MAIN), {1, 2})
+        cosines(first_x, y0, 4)
         groups = (MAIN[:9], MAIN[9:])
         results = network([packed_pair(columns) for columns in groups])
         for columns, value in zip(groups, results):
             spread(value, columns)
+        slopes_by_bond(4)
         final = []
         for sub in (0, 1):
             spin = state[1, :, sub, first_x + 1 : first_x + 3, r0 : r0 + 8, :]
@@ -458,8 +487,10 @@
             late = (slot_of == 3 + sub) & (z_of >= 64)
             final.append(jnp.where(late, jnp.where(seam, again, trial[sub]), spin))
         for sub in (0, 1):
+            send_buf[2 * h + y0, :, sub, :, :, :] = final[sub][:, :, 3 + sub : 4 + sub, :]
+        send(2 * h + y0)
+        for sub in (0, 1):
             write_targets(sub, first_x, y0, final[sub])
-            send_buf[2 * h + y0, :, sub, :, :, :] = final[sub][:, :, 3 + sub : 4 + sub, :]
 
     started = {}
 
@@ -491,14 +522,14 @@
 
     for p in range(4):
         phase(*PHASES[p])
-        send(p)
 
     for sub in (0, 1):
-        spin_out[:, sub] = state[1, :, sub, 2:6, 4 + sub : 6 + sub, :]
+        both_out[0, :, sub] = state[1, :, sub, 2:6, 4 + sub : 6 + sub, :]
     evaluate(gather(FINAL, 1, 0, (0, 0), 4))
+    slopes_by_bond(NXI)
     for sub in (0, 1):
         total = fields(sub, 1, 4, 1, 0)
-        field_out[:, sub] = total[:, :, 3 + sub : 5 + sub, :]
+        both_out[1, :, sub] = total[:, :, 3 + sub : 5 + sub, :]
 
 
 def solution(mesh):
@@ -508,18 +539,25 @@
         brick = jax.ShapeDtypeStruct(spin.shape, F32)
         vmem = pl.BlockSpec(memory_space=pltpu.VMEM)
         dma = pltpu.SemaphoreType.DMA
-        return pl.pallas_call(
+        both = pl.pallas_call(
             functools.partial(kernel, n_gx, n_yz),
-            out_shape=(brick, brick),
-            in_specs=[vmem] * 5,
-            out_specs=(vmem, vmem),
+            out_shape=jax.ShapeDtypeStruct((2,) + spin.shape, F32),
+            in_specs=[pl.BlockSpec(memory_space=pl.ANY)] * 5,
+            out_specs=vmem,
             scratch_shapes=[
                 pltpu.VMEM((3, 3, 2, 8, 16, 128), F32),
-                pltpu.VMEM(((2 * NT + 2) * 8, 128), F32),
-                pltpu.VMEM(((2 * NT + 2) * 8, 128), F32),
+                pltpu.VMEM((2, 2, NXI, 8, 8, 128), F32),
+                pltpu.VMEM((2, 2, NXI, 8, 8, 128), F32),
+                pltpu.VMEM((2, 14, NXI, 24, 128), F32),
                 pltpu.VMEM((256, 256), BF16),
                 pltpu.VMEM((256, 256), BF16),
                 pltpu.VMEM((128, 128), F32),
+                pltpu.VMEM(spin.shape, F32),
+                pltpu.VMEM(pair.shape, F32),
+                pltpu.VMEM(mix.shape, F32),
+                pltpu.VMEM((1, 128), F32),
+                pltpu.VMEM((1, 128), F32),
+                dma((5,)),
                 pltpu.VMEM((4, 3, 2, 4, 2, 128), F32),
                 pltpu.VMEM((5, 3, 2, 2, 2, 128), F32),
                 pltpu.VMEM((4, 3, 2, 2, 1, 128), F32),
@@ -531,6 +569,7 @@
             ],
             compiler_params=pltpu.CompilerParams(collective_id=0, has_side_effects=True),
         )(spin, pair, mix, bias.reshape(1, 128), out_w.reshape(1, 128))
+        return both[0], both[1]
 
     placed = (P(None, None, "gx", "yz", None), P(), P(), P(), P())
     return jax.shard_map(

time: 49 us -> 46.7 us (0.953)
  Pallas kernels: 46.2 us -> 44.6 us
  local copies, waits for them, and re-layouts: 1.96 us -> 1.38 us
    unnamed x4 -> x0, local copies, waits for them, and re-layouts: 1.96 us -> none
    pallas_call x1, Pallas kernels: 46.2 us -> 44.6 us  [per_device(): pl.pallas_call(functools.partial(kernel, n_gx, n_yz), out_shape=jax.Shape...]
    squeeze x0 -> x1, local copies, waits for them, and re-layouts: none -> 1.38 us  [per_device(): return (both[0], both[1])]
where the time goes in v2:
time: 46.7 us; the launch traced here: 46.6 us
  Pallas kernels  44.6 us (96%)
  local copies, waits for them, and re-layouts  1.38 us (3%)
  between operations  0.64 us (1%)
    pallas_call x1, Pallas kernels, per_device(): pl.pallas_call(functools.partial(kernel, n_gx, n_yz), out_shape=jax.Shape...  44.6 us
    squeeze x1, local copies, waits for them, and re-layouts, per_device(): return (both[0], both[1])  1.38 us

profile of v2, /device:TPU:1, one launch (start us, length us, event | category | flops | bytes accessed | tf_op | source)
XLA Modules:
  0.0 46.6 jit_solution(14591725113831441431)
XLA Ops:
  0.6 44.6 %shard_map.68 = f32[2,3,2,4,2,128]{5,4,3,2,1,0:T(2,128)} custom-call(f32[3,2,4,2,128]{4,3,2,1,0:T(2,128)} %spin_hbm.1, f32[112,128]{1,0:T(8,128)} %pair_hbm.1, f32[128,128]{1,0:T(8,128)} %mix_hbm.1, f32[1,128]{1,0:T(1,128)} %bitcast.6, f32[1,128]{1,0:T(1,128)} %bitcast.7), custom_call_target="tpu_custom_call" | custom-call | tf_op jit(solution)/shard_map/pallas_call | solution.py:542
  45.2 1.4 %slice_bitcast_fusion = (f32[3,2,4,2,128]{4,3,2,1,0:T(2,128)}, f32[3,2,4,2,128]{4,3,2,1,0:T(2,128)}) fusion(f32[2,3,2,4,2,128]{5,4,3,2,1,0:T(2,128)} %shard_map.68), kind=kLoop, calls=%fused_computation | loop fusion | bytes 98304 | tf_op jit(solution)/shard_map/squeeze | solution.py:572

commit v3 on v2

--- a/solution.py
+++ b/solution.py
@@ -264,20 +264,20 @@
         put(lambda sub: start_gx[j, :, sub], 0, 2, -2 * d, 2)
     roll_all(0, 6)
 
-    def cosines(first_x, y0, count):
-        r0 = 1 + y0
-        for sub in (0, 1):
-            centre = state[1, :, sub, first_x : first_x + count, r0 : r0 + 8]
+    def cosines(first_x, y0, low, high):
+        r0, count = 1 + y0, high - low
+        for sub in (0, 1):
+            centre = state[1, :, sub, first_x + low : first_x + high, r0 : r0 + 8]
             for half in (0, 1):
                 values = []
                 for target, dx, dy, dz in BONDS[sub][8 * half : 8 * half + 8]:
-                    r, x = r0 + row_shift(sub, target, dy), first_x + dx
+                    r, x = r0 + row_shift(sub, target, dy), first_x + low + dx
                     product = centre * state[1 + dz, :, target, x : x + count, r : r + 8]
                     values.append(product[0] + product[1] + product[2])
                 values += [jnp.ones((count, 8, 128), F32)] * (8 - len(values))
                 for slot, value in enumerate(exchange(values)):
                     if 1 <= slot <= 6:
-                        cosine[half, sub, 0:count, slot] = value
+                        cosine[half, sub, low:high, slot] = value
 
     def load_cosine(column):
         sub, x, y = column
@@ -290,12 +290,17 @@
 
     def slopes_by_bond(count):
         for sub in (0, 1):
-            for half in (0, 1):
-                zero = jnp.zeros((count, 8, 128), F32)
-                values = [zero] + [slope[half, sub, 0:count, slot] for slot in range(1, 7)] + [zero]
-                for o, value in enumerate(exchange(values)):
+            for half, low, high in ((0, 1 - sub, count - sub), (1, 1, count - 1)):
+                zero = jnp.zeros((high - low, 8, 128), F32)
+                values = [slope[half, sub, low:high, slot] for slot in range(1, 7)]
+                for o, value in enumerate(exchange([zero] + values + [zero])):
                     if 8 * half + o < 14:
-                        by_bond[sub, 8 * half + o, 0:count, 8:16, :] = value
+                        by_bond[sub, 8 * half + o, low:high, 8:16, :] = value
+            for o, xi in ((0, 0), (1, count - 1)):
+                for slot in range(1, 7):
+                    by_bond[sub, 8 + o, xi, 8 + slot : 9 + slot, :] = slope[
+                        1, sub, xi, slot, o : o + 1, :
+                    ]
 
     def product(weight, value):
         high = value.astype(BF16)
@@ -427,28 +432,35 @@
 
     def gather(columns, first_x, y0, origin, reader):
         count = 4 if reader < 4 else NXI
+        cosines_of = functools.partial(cosines, first_x, y0)
         if reader == 0:
-            cosines(first_x, y0, count)
+            cosines_of(0, count)
             return columns
-        arriving = set()
-        for p in range(reader):
+        for p in range(reader - 1):
             for source in ORDERED[p]:
                 if SOURCES[p][source] == reader:
-                    if p < reader - 1:
-                        receive(p, source)
-                    else:
-                        arriving |= message_places(*PHASES[p], *source)
-        for p in range(reader - 1):
-            reroll(p, reader)
-        early, late = split(columns, arriving, origin)
-        cosines(first_x, y0, count)
-        evaluate(early)
-        for source in ORDERED[reader - 1]:
-            if SOURCES[reader - 1][source] == reader:
-                receive(reader - 1, source)
-        reroll(reader - 1, reader)
-        cosines(first_x, y0, count)
-        return late
+                    receive(p, source)
+            reroll(p, reader, (0, 1, -1))
+        p = reader - 1
+        tiers = []
+        late = [d for d in ORDERED[p] if SOURCES[p][d] == reader]
+        if reader in (1, 3):
+            parts = ([(0, 1)], [d for d in late if d != (0, 1)])
+        else:
+            parts = ([d for d in late if d[0] == 0], [d for d in late if d[0] != 0])
+        for found in parts:
+            places = set().union(*[message_places(*PHASES[p], *d) for d in found])
+            tiers.append((found, places, {d[0] for d in found}))
+        cosines_of(0, count)
+        for step, (found, places, sides) in enumerate(tiers):
+            ready, columns = split(columns, set().union(*[t[1] for t in tiers[step:]]), origin)
+            evaluate(ready)
+            for source in found:
+                receive(p, source)
+            reroll(p, reader, sides)
+            touched = [x + 2 - first_x for x, _ in places]
+            cosines_of(max(0, min(touched) - 1), min(count, max(touched) + 2))
+        return columns
 
     def phase(h, y0):
         x0 = 2 * h
@@ -474,7 +486,7 @@
                 extra = (slot_of == 2) & (z_of == 63)
             change = ((slot_of == 3 + sub) & (z_of < 64)) | extra
             write_targets(sub, first_x, y0, jnp.where(change, trial[sub], old[sub]))
-        cosines(first_x, y0, 4)
+        cosines(first_x, y0, 0, 4)
         groups = (MAIN[:9], MAIN[9:])
         results = network([packed_pair(columns) for columns in groups])
         for columns, value in zip(groups, results):
@@ -514,9 +526,9 @@
         dgx, e = source
         put(lambda sub: got[p, j, :, sub], 4 * dgx + 2 * h + 2, 2, y0 + 2 * e, 1)
 
-    def reroll(p, reader):
+    def reroll(p, reader, sides):
         h, _ = PHASES[p]
-        for dgx in (0, 1, -1):
+        for dgx in sides:
             if any(d[0] == dgx and SOURCES[p][d] == reader for d in ORDERED[p]):
                 roll_all(4 * dgx + 2 * h + 2, 2)
 

time: 46.7 us -> 45.6 us (0.976)
  Pallas kernels: 44.6 us -> 43.2 us
    pallas_call x1, Pallas kernels: 44.6 us -> 43.2 us  [per_device(): pl.pallas_call(functools.partial(kernel, n_gx, n_yz), out_shape=jax.Shape...]
where the time goes in v3:
time: 45.6 us; the launch traced here: 45.2 us
  Pallas kernels  43.2 us (95%)
  local copies, waits for them, and re-layouts  1.38 us (3%)
  between operations  0.64 us (1%)
    pallas_call x1, Pallas kernels, per_device(): pl.pallas_call(functools.partial(kernel, n_gx, n_yz), out_shape=jax.Shape...  43.2 us
    squeeze x1, local copies, waits for them, and re-layouts, per_device(): return (both[0], both[1])  1.38 us

profile of v3, /device:TPU:1, one launch (start us, length us, event | category | flops | bytes accessed | tf_op | source)
XLA Modules:
  0.0 45.2 jit_solution(695817516566251353)
XLA Ops:
  0.6 43.2 %shard_map.68 = f32[2,3,2,4,2,128]{5,4,3,2,1,0:T(2,128)} custom-call(f32[3,2,4,2,128]{4,3,2,1,0:T(2,128)} %spin_hbm.1, f32[112,128]{1,0:T(8,128)} %pair_hbm.1, f32[128,128]{1,0:T(8,128)} %mix_hbm.1, f32[1,128]{1,0:T(1,128)} %bitcast.6, f32[1,128]{1,0:T(1,128)} %bitcast.7), custom_call_target="tpu_custom_call" | custom-call | tf_op jit(solution)/shard_map/pallas_call | solution.py:554
  43.8 1.4 %slice_bitcast_fusion = (f32[3,2,4,2,128]{4,3,2,1,0:T(2,128)}, f32[3,2,4,2,128]{4,3,2,1,0:T(2,128)}) fusion(f32[2,3,2,4,2,128]{5,4,3,2,1,0:T(2,128)} %shard_map.68), kind=kLoop, calls=%fused_computation | loop fusion | bytes 98304 | tf_op jit(solution)/shard_map/squeeze | solution.py:584

commit v4 on v3

--- a/solution.py
+++ b/solution.py
@@ -12,7 +12,7 @@
 NB = 8
 NXI = 6
 TIME_STEP = 0.1
-CHUNK = 2
+CHUNK = 20
 F32 = jnp.float32
 BF16 = jnp.bfloat16
 
@@ -207,15 +207,15 @@
     for j, d in enumerate(GX_DELTAS):
         starts.append(
             pltpu.make_async_remote_copy(
-                src_ref=spin_hbm.at[:, :, 2:4],
-                dst_ref=start_gx.at[j],
+                src_ref=spin_hbm.at[:, :, (3 if abs(d) == 2 else 2) : 4],
+                dst_ref=start_gx.at[j, :, :, (1 if abs(d) == 2 else 0) : 2],
                 send_sem=start_send.at[4 + j],
                 recv_sem=start_recv.at[4 + j],
                 device_id=device(1, d),
                 device_id_type=MESH,
             )
         )
-    for copy in starts:
+    for copy in starts[:3:-1] + starts[:4]:
         copy.start()
 
     for load in loads:
@@ -261,7 +261,8 @@
     for j, d in enumerate(DELTAS):
         put(lambda sub: start_yz[j, :, sub], 2, 4, -2 * d, 2)
     for j, d in enumerate(GX_DELTAS):
-        put(lambda sub: start_gx[j, :, sub], 0, 2, -2 * d, 2)
+        first = 1 if abs(d) == 2 else 0
+        put(lambda sub: start_gx[j, :, sub, first:], first, 2 - first, -2 * d, 2)
     roll_all(0, 6)
 
     def cosines(first_x, y0, low, high):

time: 45.6 us -> 44.7 us (0.980)
  Pallas kernels: 43.2 us -> 42.5 us
    pallas_call x1, Pallas kernels: 43.2 us -> 42.5 us  [per_device(): pl.pallas_call(functools.partial(kernel, n_gx, n_yz), out_shape=jax.Shape...]
where the time goes in v4:
time: 44.7 us; the launch traced here: 44.5 us
  Pallas kernels  42.5 us (95%)
  local copies, waits for them, and re-layouts  1.38 us (3%)
  between operations  0.64 us (1%)
    pallas_call x1, Pallas kernels, per_device(): pl.pallas_call(functools.partial(kernel, n_gx, n_yz), out_shape=jax.Shape...  42.5 us
    squeeze x1, local copies, waits for them, and re-layouts, per_device(): return (both[0], both[1])  1.38 us

profile of v4, /device:TPU:1, one launch (start us, length us, event | category | flops | bytes accessed | tf_op | source)
XLA Modules:
  0.0 44.5 jit_solution(6368591875635954784)
XLA Ops:
  0.6 42.5 %shard_map.68 = f32[2,3,2,4,2,128]{5,4,3,2,1,0:T(2,128)} custom-call(f32[3,2,4,2,128]{4,3,2,1,0:T(2,128)} %spin_hbm.1, f32[112,128]{1,0:T(8,128)} %pair_hbm.1, f32[128,128]{1,0:T(8,128)} %mix_hbm.1, f32[1,128]{1,0:T(1,128)} %bitcast.6, f32[1,128]{1,0:T(1,128)} %bitcast.7), custom_call_target="tpu_custom_call" | custom-call | tf_op jit(solution)/shard_map/pallas_call | solution.py:555
  43.1 1.4 %slice_bitcast_fusion = (f32[3,2,4,2,128]{4,3,2,1,0:T(2,128)}, f32[3,2,4,2,128]{4,3,2,1,0:T(2,128)}) fusion(f32[2,3,2,4,2,128]{5,4,3,2,1,0:T(2,128)} %shard_map.68), kind=kLoop, calls=%fused_computation | loop fusion | bytes 98304 | tf_op jit(solution)/shard_map/squeeze | solution.py:585

commit v5 on v4

--- a/solution.py
+++ b/solution.py
@@ -171,7 +171,7 @@
 
     barrier = pltpu.get_barrier_semaphore()
     partners = [(0, d) for d in DELTAS] + [(s, d) for s in (1, -1) for d in GX_DELTAS]
-    for dgx, dyz in partners:
+    for dgx, dyz in partners[::-1]:
         pl.semaphore_signal(barrier, inc=1, device_id=device(dgx, dyz), device_id_type=MESH)
 
     loads = []
@@ -187,8 +187,6 @@
         load = pltpu.make_async_copy(source, target, load_sem.at[j])
         load.start()
         loads.append(load)
-    slope[...] = jnp.zeros(slope.shape, F32)
-    state[...] = jnp.zeros(state.shape, F32)
 
     pl.semaphore_wait(barrier, len(partners))
 
@@ -217,6 +215,8 @@
         )
     for copy in starts[:3:-1] + starts[:4]:
         copy.start()
+    slope[...] = jnp.zeros(slope.shape, F32)
+    state[...] = jnp.zeros(state.shape, F32)
 
     for load in loads:
         load.wait()

time: 44.7 us -> 44.6 us (level)
  no operation moved by 1% of the time
where the time goes in v5:
time: 44.6 us; the launch traced here: 44.5 us
  Pallas kernels  42.5 us (95%)
  local copies, waits for them, and re-layouts  1.38 us (3%)
  between operations  0.64 us (1%)
    pallas_call x1, Pallas kernels, per_device(): pl.pallas_call(functools.partial(kernel, n_gx, n_yz), out_shape=jax.Shape...  42.5 us
    squeeze x1, local copies, waits for them, and re-layouts, per_device(): return (both[0], both[1])  1.38 us

profile of v5, /device:TPU:1, one launch (start us, length us, event | category | flops | bytes accessed | tf_op | source)
XLA Modules:
  0.0 44.5 jit_solution(15360242904911026547)
XLA Ops:
  0.6 42.5 %shard_map.68 = f32[2,3,2,4,2,128]{5,4,3,2,1,0:T(2,128)} custom-call(f32[3,2,4,2,128]{4,3,2,1,0:T(2,128)} %spin_hbm.1, f32[112,128]{1,0:T(8,128)} %pair_hbm.1, f32[128,128]{1,0:T(8,128)} %mix_hbm.1, f32[1,128]{1,0:T(1,128)} %bitcast.6, f32[1,128]{1,0:T(1,128)} %bitcast.7), custom_call_target="tpu_custom_call" | custom-call | tf_op jit(solution)/shard_map/pallas_call | solution.py:555
  43.1 1.4 %slice_bitcast_fusion = (f32[3,2,4,2,128]{4,3,2,1,0:T(2,128)}, f32[3,2,4,2,128]{4,3,2,1,0:T(2,128)}) fusion(f32[2,3,2,4,2,128]{5,4,3,2,1,0:T(2,128)} %shard_map.68), kind=kLoop, calls=%fused_computation | loop fusion | bytes 98304 | tf_op jit(solution)/shard_map/squeeze | solution.py:585
